TPU v7x, 32 devices: a whole 2x2x4 slice. The times are simulated.
32 devices in a mesh: row: 4 (over y, x), col: 8 (over z, core).
Axes of the slice: x: 2, y: 2, z: 4, core: 2. Of those that a mesh axis runs over, the one named last changes fastest.
Arguments:
- tokens: bfloat16 [256, 8192], P('col', 'row'), may hold values from -500 to 500
- norm_gain: float32 [8192], P('row'), may hold values from 0.5 to 1.5
- cotangent: bfloat16 [256, 8192], P('col', 'row'), may hold values from -6 to 6
- gate_frozen_weight: bfloat16 [8192, 28672], P('row', 'col'), may hold values from -0.0625 to 0.0625
- up_frozen_weight: bfloat16 [8192, 28672], P('row', 'col'), may hold values from -0.0625 to 0.0625
- down_frozen_weight: bfloat16 [28672, 8192], P('col', 'row'), may hold values from -0.03125 to 0.03125
- gate_input_factor: bfloat16 [8192, 64], P('row'), may hold values from -0.0625 to 0.0625
- gate_output_factor: bfloat16 [64, 28672], P(None, 'col'), may hold values from -0.75 to 0.75
- up_input_factor: bfloat16 [8192, 64], P('row'), may hold values from -0.0625 to 0.0625
- up_output_factor: bfloat16 [64, 28672], P(None, 'col'), may hold values from -0.75 to 0.75
- down_input_factor: bfloat16 [28672, 64], P('col'), may hold values from -0.03125 to 0.03125
- down_b: bfloat16 [64, 8192], P(None, 'row'), may hold values from -0.75 to 0.75
- gate_input_factor_direction: bfloat16 [8192, 64], P('row'), may hold values from -0.0625 to 0.0625
- gate_output_factor_direction: bfloat16 [64, 28672], P(None, 'col'), may hold values from -0.75 to 0.75
- up_input_factor_direction: bfloat16 [8192, 64], P('row'), may hold values from -0.0625 to 0.0625
- up_output_factor_direction: bfloat16 [64, 28672], P(None, 'col'), may hold values from -0.75 to 0.75
- down_input_factor_direction: bfloat16 [28672, 64], P('col'), may hold values from -0.03125 to 0.03125
- down_b_dir: bfloat16 [64, 8192], P(None, 'row'), may hold values from -0.75 to 0.75
Outputs:
- normed_feature_adjoint: float32 [256, 8192], P('col', 'row')
- normed_feature_adjoint_direction: float32 [256, 8192], P('col', 'row')
- curvature_gate_input: float32 [8192, 64], P('row')
- curvature_gate_output: float32 [64, 28672], P(None, 'col')
- curvature_up_input: float32 [8192, 64], P('row')
- curvature_up_output: float32 [64, 28672], P(None, 'col')
- curvature_down_input: float32 [28672, 64], P('col')
- curvature_down_output: float32 [64, 8192], P(None, 'row')
All inputs are finite; a program needn't handle non-finite values.
Results may differ from a plain program's by a relative error of at most 0.024.
Values may be sent and summed in bfloat16 or wider, within the bound.
A program may use at most 128 MiB of HBM per device.

v0:
```python
import jax
import jax.numpy as jnp
from jax import lax
from jax.sharding import PartitionSpec as P

D = 8192
adapter_scale = 0.5
epsilon = 1e-05


def curvature_product(left, right):
    return jnp.dot(left, right, preferred_element_type=jnp.float32)


def cross_shard_total(left, right):
    return lax.dot_general(
        left, right, (((1,), (1,)), ((), ())), preferred_element_type=jnp.float32
    )


def summed_over_rows(left, right):
    return lax.dot_general(
        left, right, (((0,), (0,)), ((), ())), preferred_element_type=jnp.float32
    )


def lowered(factor, panel):
    return lax.dot_general(
        factor, panel, (((0,), (1,)), ((), ())), preferred_element_type=jnp.float32
    )


def lifted(adjoint, factor):
    return lax.dot_general(
        adjoint, factor, (((0,), (1,)), ((), ())), precision=lax.Precision.HIGHEST
    )


def second_order(
    gate_preactivation,
    up_preactivation,
    hidden_adjoint,
    gate_tangent_rows,
    up_tangent_rows,
    adjoint_tangent_rows,
):
    sigma = jax.nn.sigmoid(gate_preactivation)
    silu_value = gate_preactivation * sigma
    slope = sigma * (1.0 + gate_preactivation * (1.0 - sigma))
    bend = sigma * (1.0 - sigma) * (2.0 + gate_preactivation * (1.0 - 2.0 * sigma))
    hidden_activation = (silu_value * up_preactivation).astype(jnp.bfloat16)
    hidden_direction = (
        slope * gate_tangent_rows * up_preactivation + silu_value * up_tangent_rows
    ).astype(jnp.bfloat16)
    gate_derivative = (hidden_adjoint * up_preactivation * slope).astype(jnp.bfloat16)
    up_derivative = (hidden_adjoint * silu_value).astype(jnp.bfloat16)
    gate_derivative_direction = (
        adjoint_tangent_rows * up_preactivation * slope
        + hidden_adjoint * (up_tangent_rows * slope + up_preactivation * bend * gate_tangent_rows)
    ).astype(jnp.bfloat16)
    up_derivative_direction = (
        adjoint_tangent_rows * silu_value + hidden_adjoint * slope * gate_tangent_rows
    ).astype(jnp.bfloat16)
    return (
        hidden_activation,
        hidden_direction,
        gate_derivative,
        up_derivative,
        gate_derivative_direction,
        up_derivative_direction,
    )


def on_device(
    tokens,
    norm_gain,
    cotangent,
    gate_frozen_weight,
    up_frozen_weight,
    down_frozen_weight,
    gate_input_factor,
    gate_output_factor,
    up_input_factor,
    up_output_factor,
    down_input_factor,
    down_b,
    gate_input_factor_direction,
    gate_output_factor_direction,
    up_input_factor_direction,
    up_output_factor_direction,
    down_input_factor_direction,
    down_b_dir,
):
    rank_size = gate_input_factor.shape[1]
    width_rows = gate_frozen_weight.shape[0]
    width_columns = gate_frozen_weight.shape[1]
    own_count = tokens.shape[0]
    tokens_f = tokens.astype(jnp.float32)
    squares = lax.psum(jnp.sum(tokens_f * tokens_f, axis=1), "row")
    own_normed = (tokens_f * lax.rsqrt(squares[:, None] / D + epsilon) * norm_gain).astype(
        jnp.bfloat16
    )
    normed_tokens, cot_panel = (
        lax.all_gather(own_normed, "col", axis=0, tiled=True),
        lax.all_gather(cotangent, "col", axis=0, tiled=True),
    )
    in_factors = jnp.concatenate(
        [
            gate_input_factor,
            up_input_factor,
            gate_input_factor_direction,
            up_input_factor_direction,
        ],
        axis=1,
    )
    out_factors = jnp.concatenate([down_b, down_b_dir], axis=0)
    projected = jnp.concatenate(
        [curvature_product(normed_tokens, in_factors), cross_shard_total(cot_panel, out_factors)],
        axis=1,
    )
    ranks = lax.psum(projected, "row").astype(jnp.bfloat16)
    swiglu_block = lax.psum(
        jnp.concatenate(
            [
                curvature_product(normed_tokens, gate_frozen_weight),
                curvature_product(normed_tokens, up_frozen_weight),
                cross_shard_total(cot_panel, down_frozen_weight),
            ],
            axis=1,
        ),
        "row",
    )

    def column(array, index):
        return array[:, index * rank_size : (index + 1) * rank_size]

    (
        gate_rank_rows,
        up_rank_rows,
        gate_rank_rows_direction,
        up_rank_rows_direction,
        adjoint_rank_rows,
        adjoint_rank_rows_direction,
    ) = [column(ranks, index) for index in range(6)]
    gate_preactivation = swiglu_block[:, :width_columns] + adapter_scale * curvature_product(
        gate_rank_rows, gate_output_factor
    )
    up_preactivation = swiglu_block[
        :, width_columns : 2 * width_columns
    ] + adapter_scale * curvature_product(up_rank_rows, up_output_factor)
    hidden_adjoint = swiglu_block[:, 2 * width_columns :] + adapter_scale * cross_shard_total(
        adjoint_rank_rows, down_input_factor
    )
    gate_tangent_rows = adapter_scale * (
        curvature_product(gate_rank_rows_direction, gate_output_factor)
        + curvature_product(gate_rank_rows, gate_output_factor_direction)
    )
    up_tangent_rows = adapter_scale * (
        curvature_product(up_rank_rows_direction, up_output_factor)
        + curvature_product(up_rank_rows, up_output_factor_direction)
    )
    adjoint_tangent_rows = adapter_scale * (
        cross_shard_total(adjoint_rank_rows_direction, down_input_factor)
        + cross_shard_total(adjoint_rank_rows, down_input_factor_direction)
    )
    (
        hidden_activation,
        hidden_direction,
        gate_derivative,
        up_derivative,
        gate_derivative_direction,
        up_derivative_direction,
    ) = second_order(
        gate_preactivation,
        up_preactivation,
        hidden_adjoint,
        gate_tangent_rows,
        up_tangent_rows,
        adjoint_tangent_rows,
    )
    (
        gate_full_rows,
        up_full_rows,
        gate_full_rows_direction,
        up_full_rows_direction,
        adjoint_full_rows,
        adjoint_full_rows_direction,
    ) = [column(ranks, index) for index in range(6)]
    curvature_gate_output = adapter_scale * (
        summed_over_rows(gate_full_rows_direction, gate_derivative)
        + summed_over_rows(gate_full_rows, gate_derivative_direction)
    )
    curvature_up_output = adapter_scale * (
        summed_over_rows(up_full_rows_direction, up_derivative)
        + summed_over_rows(up_full_rows, up_derivative_direction)
    )
    curvature_down_input = adapter_scale * (
        summed_over_rows(hidden_direction, adjoint_full_rows)
        + summed_over_rows(hidden_activation, adjoint_full_rows_direction)
    )
    rank_adjoints = jnp.concatenate(
        [
            cross_shard_total(gate_output_factor, gate_derivative),
            cross_shard_total(up_output_factor, up_derivative),
            cross_shard_total(gate_output_factor, gate_derivative_direction)
            + cross_shard_total(gate_output_factor_direction, gate_derivative),
            cross_shard_total(up_output_factor, up_derivative_direction)
            + cross_shard_total(up_output_factor_direction, up_derivative),
            lowered(down_input_factor, hidden_direction)
            + lowered(down_input_factor_direction, hidden_activation),
        ],
        axis=0,
    )
    factors_f = [
        factor.astype(jnp.float32)
        for factor in (
            gate_input_factor,
            up_input_factor,
            gate_input_factor_direction,
            up_input_factor_direction,
        )
    ]
    normed_f = normed_tokens.astype(jnp.float32)
    cotangent_float = cot_panel.astype(jnp.float32)
    adjoints = lax.psum(rank_adjoints.astype(jnp.bfloat16), "col").astype(jnp.float32)
    adjoint_contribution = cross_shard_total(
        gate_derivative, gate_frozen_weight
    ) + cross_shard_total(up_derivative, up_frozen_weight)
    tangent_contribution = cross_shard_total(
        gate_derivative_direction, gate_frozen_weight
    ) + cross_shard_total(up_derivative_direction, up_frozen_weight)
    adjoint_contribution, tangent_contribution = (adjoint_contribution, tangent_contribution)
    summed = lax.psum_scatter(
        jnp.concatenate([adjoint_contribution, tangent_contribution], axis=1).astype(jnp.bfloat16),
        "col",
        scatter_dimension=0,
        tiled=True,
    ).astype(jnp.float32)
    normed_feature_adjoint = summed[:, :width_rows]
    normed_feature_adjoint_direction = summed[:, width_rows:]
    piece = lax.dynamic_slice_in_dim(adjoints, lax.axis_index("col") * own_count, own_count, 1)
    parts = [piece[index * rank_size : (index + 1) * rank_size] for index in range(5)]
    adjoint_contribution = lifted(parts[0], factors_f[0]) + lifted(parts[1], factors_f[1])
    tangent_contribution = (
        lifted(parts[2], factors_f[0])
        + lifted(parts[0], factors_f[2])
        + lifted(parts[3], factors_f[1])
        + lifted(parts[1], factors_f[3])
    )
    normed_feature_adjoint = normed_feature_adjoint + adapter_scale * adjoint_contribution
    normed_feature_adjoint_direction = (
        normed_feature_adjoint_direction + adapter_scale * tangent_contribution
    )
    spread = (((0,), (1,)), ((), ()))
    gate_dir_rows = adjoints[2 * rank_size : 3 * rank_size]
    up_dir_rows = adjoints[3 * rank_size : 4 * rank_size]
    rank_row_values = adjoints[4 * rank_size : 5 * rank_size]
    gate_contribution = adapter_scale * lax.dot_general(
        normed_f, gate_dir_rows, spread, precision=lax.Precision.HIGHEST
    )
    up_contribution = adapter_scale * lax.dot_general(
        normed_f, up_dir_rows, spread, precision=lax.Precision.HIGHEST
    )
    down_contribution = adapter_scale * jnp.dot(
        rank_row_values, cotangent_float, precision=lax.Precision.HIGHEST
    )
    return (
        normed_feature_adjoint,
        normed_feature_adjoint_direction,
        gate_contribution,
        curvature_gate_output,
        up_contribution,
        curvature_up_output,
        curvature_down_input,
        down_contribution,
    )


def solution(mesh):
    in_specs = (
        P("col", "row"),
        P("row"),
        P("col", "row"),
        P("row", "col"),
        P("row", "col"),
        P("col", "row"),
        P("row", None),
        P(None, "col"),
        P("row", None),
        P(None, "col"),
        P("col", None),
        P(None, "row"),
        P("row", None),
        P(None, "col"),
        P("row", None),
        P(None, "col"),
        P("col", None),
        P(None, "row"),
    )
    out_specs = (
        P("col", "row"),
        P("col", "row"),
        P("row", None),
        P(None, "col"),
        P("row", None),
        P(None, "col"),
        P("col", None),
        P(None, "row"),
    )
    return jax.shard_map(
        on_device, mesh=mesh, in_specs=in_specs, out_specs=out_specs, check_vma=False
    )
```

profile of v0, /device:TPU:0, one launch (start us, length us, event | category | flops | bytes accessed | tf_op | source)
XLA Modules:
  0.0 468.7 jit_solution(18091516543193688266)
XLA Ops:
  8.3 11.4 %psum.28 = f32[32]{0:T(128)S(1)} all-reduce(f32[32]{0:T(128)S(1)} %fusion.49), channel_id=1, replica_groups=mesh['row'=4,'col'=8] {'row'}, use_global_device_ids=true, to_apply=%region_1.0 | all-reduce | flops 32 | bytes 256 | tf_op jit(solution)/shard_map/psum | solution.py:99
  22.2 21.0 %all-gather.3.cloned.1.call-done = bf16[256,2048]{1,0:T(8,128)(2,1)} async-done(((bf16[32,2048]{1,0:T(8,128)(2,1)}), bf16[256,2048]{1,0:T(8,128)(2,1)}) %all-gather.3.cloned.1.call-update) | async-done | bytes 1048592 | tf_op jit(solution)/shard_map/all_gather | solution.py:104
  43.2 11.5 %fusion.88 = f32[256,3584]{1,0:T(8,128)} fusion(bf16[256,2048]{1,0:T(8,128)(2,1)} %all-gather.3.cloned.1.call-done, bf16[2048,3584]{1,0:T(8,128)(2,1)} %param.21), kind=kOutput, calls=%fused_computation.126 | convolution fusion | flops 3758096384 | bytes 19398656 | tf_op jit(solution)/shard_map/dot_general | solution.py:12
  54.6 9.2 %fusion.89 = f32[256,3584]{1,0:T(8,128)} fusion(bf16[256,2048]{1,0:T(8,128)(2,1)S(1)} %copy-done.10, bf16[2048,3584]{1,0:T(8,128)(2,1)} %param.22), kind=kOutput, calls=%fused_computation.127 | convolution fusion | flops 3758096384 | bytes 19398656 | tf_op jit(solution)/shard_map/dot_general | solution.py:12
  63.8 2.8 all-gather.5.cloned.1.call-done
  66.6 11.4 %fusion.90 = f32[256,3584]{1,0:T(8,128)} fusion(bf16[256,2048]{1,0:T(8,128)(2,1)} %all-gather.5.cloned.1.call-done, bf16[3584,2048]{1,0:T(8,128)(2,1)} %param.23), kind=kOutput, calls=%fused_computation.128 | convolution fusion | flops 3758096384 | bytes 19398656 | tf_op jit(solution)/shard_map/dot_general | solution.py:16
  78.0 7.5 %pad_maximum_fusion = f32[256,10752]{1,0:T(8,128)} fusion(f32[256,3584]{1,0:T(8,128)} %fusion.90, f32[256,3584]{1,0:T(8,128)} %fusion.89, f32[256,3584]{1,0:T(8,128)S(1)} %copy-done.17), kind=kLoop, calls=%fused_computation | loop fusion | flops 5505024 | bytes 22020096 | tf_op jit(solution)/shard_map/concatenate | solution.py:123
  89.9 35.4 %all-reduce.7 = bf16[256,384]{0,1:T(8,128)(2,1)S(1)} all-reduce(f32[256,384]{0,1:T(8,128)S(1)} %pad_maximum_fusion.2), channel_id=1, replica_groups=mesh['row'=4,'col'=8] {'row'}, use_global_device_ids=true, to_apply=%region_3.0 | all-reduce | flops 98304 | bytes 589824 | tf_op jit(solution)/shard_map/psum | solution.py:121
  126.6 2.5 fusion.61
  129.1 2.5 fusion
  131.6 2.5 fusion.2
  134.1 178.0 %all-reduce.4.cloned.1.call-done = f32[256,10752]{1,0:T(8,128)} async-done(((f32[256,10752]{1,0:T(8,128)}), f32[256,10752]{1,0:T(8,128)}) %all-reduce.4.cloned.1.call-update) | async-done | bytes 11010064 | tf_op jit(solution)/shard_map/psum | solution.py:122
  312.1 4.5 fusion.3
  316.6 4.7 %fusion.5 = f32[256,3584]{1,0:T(8,128)} fusion(bf16[3584,64]{0,1:T(8,128)(2,1)S(1)} %copy-done.12, f32[256,10752]{1,0:T(8,128)} %all-reduce.4.cloned.1.call-done, bf16[256,384]{0,1:T(8,128)(2,1)S(1)} %all-reduce.7), kind=kOutput, calls=%fused_computation.12 | convolution fusion | flops 119275520 | bytes 7831552 | tf_op jit(solution)/shard_map/dot_general | solution.py:16
  321.3 4.7 %fusion.4 = f32[256,3584]{1,0:T(8,128)} fusion(bf16[64,3584]{1,0:T(8,128)(2,1)S(1)} %copy-done.9, f32[256,10752]{1,0:T(8,128)} %all-reduce.4.cloned.1.call-done, bf16[256,384]{0,1:T(8,128)(2,1)S(1)} %all-reduce.7), kind=kOutput, calls=%fused_computation.10 | convolution fusion | flops 119275520 | bytes 7831552 | tf_op jit(solution)/shard_map/dot_general | solution.py:12
  326.5 9.5 %add_convert_fusion = (bf16[256,3584]{1,0:T(8,128)(2,1)}, bf16[256,3584]{1,0:T(8,128)(2,1)S(1)}, bf16[256,3584]{1,0:T(8,128)(2,1)}, bf16[256,3584]{1,0:T(8,128)(...) fusion(f32[256,3584]{1,0:T(8,128)} %fusion.4, f32[256,3584]{1,0:T(8,128)S(1)} %copy-done.15, ...), kind=kOutput, calls=%fused_computation.31 | convolution fusion | flops 155975680 | bytes 33521664 | tf_op jit(solution)/shard_map/dot_general | solution.py:12
  337.9 8.6 %fusion.91 = f32[256,2048]{1,0:T(8,128)} fusion(bf16[256,3584]{1,0:T(8,128)(2,1)S(1)} %get-tuple-element.11, bf16[2048,3584]{1,0:T(8,128)(2,1)} %param.21), kind=kOutput, calls=%fused_computation.129 | convolution fusion | flops 3758096384 | bytes 18612224 | tf_op jit(solution)/shard_map/dot_general | solution.py:16
  347.2 8.7 %fusion.92 = f32[256,2048]{1,0:T(8,128)} fusion(bf16[256,3584]{1,0:T(8,128)(2,1)S(1)} %get-tuple-element.9, bf16[2048,3584]{1,0:T(8,128)(2,1)} %param.21), kind=kOutput, calls=%fused_computation.130 | convolution fusion | flops 3758096384 | bytes 18612224 | tf_op jit(solution)/shard_map/dot_general | solution.py:16
  355.9 2.2 fusion.94
  365.8 10.3 %fusion.19 = bf16[256,2048]{1,0:T(8,128)(2,1)S(1)} fusion(f32[256,2048]{1,0:T(8,128)} %fusion.91, bf16[256,3584]{1,0:T(8,128)(2,1)} %copy-done.1, bf16[2048,3584]{1,0:T(8,128)(2,1)} %param.22), kind=kOutput, calls=%fused_computation.39 | convolution fusion | flops 3759144960 | bytes 19660800 | tf_op jit(solution)/shard_map/dot_general | solution.py:16
  376.1 11.3 %fusion.20 = bf16[256,2048]{1,0:T(8,128)(2,1)} fusion(f32[256,2048]{1,0:T(8,128)} %fusion.92, bf16[256,3584]{1,0:T(8,128)(2,1)} %get-tuple-element.10, bf16[2048,3584]{1,0:T(8,128)(2,1)} %param.22), kind=kOutput, calls=%fused_computation.40 | convolution fusion | flops 3759144960 | bytes 19660800 | tf_op jit(solution)/shard_map/dot_general | solution.py:16
  387.4 2.8 pad_maximum_fusion.1
  397.4 20.9 %all-reduce.6.cloned.1.call-done = bf16[320,256]{1,0:T(8,128)(2,1)} async-done(((bf16[320,256]{1,0:T(8,128)(2,1)}), bf16[320,256]{1,0:T(8,128)(2,1)}) %all-reduce.6.cloned.1.call-update) | async-done | bytes 163856 | tf_op jit(solution)/shard_map/psum | solution.py:225
  426.8 31.5 %reduce-scatter.2.cloned.1.call-done = bf16[32,4096]{1,0:T(8,128)(2,1)} async-done(((bf16[256,4096]{1,0:T(8,128)(2,1)}), bf16[32,4096]{1,0:T(8,128)(2,1)}) %reduce-scatter.2.cloned.1.call-update) | async-done | bytes 262160 | tf_op jit(solution)/shard_map/reduce_scatter | solution.py:233
  (101 shorter events, 39.3 us)
Async XLA Ops:
  7.2 318.9 %copy-start = (bf16[64,3584]{1,0:T(8,128)(2,1)S(1)}, bf16[64,3584]{1,0:T(8,128)(2,1)}, u32[]{:S(2)}) copy-start(bf16[64,3584]{1,0:T(8,128)(2,1)} %param.33) | copy-start | bytes 1376260
  7.2 36.0 %all-gather.3.cloned.1.call-start = ((), (), s32[]{:S(2)}) async-start(), calls=%async_computation.1 | async-start | bytes 1179648 | tf_op jit(solution)/shard_map/all_gather | solution.py:104
  21.4 45.2 %all-gather.5.cloned.1.call-start = ((), (), s32[]{:S(2)}) async-start(), calls=%async_computation.2 | async-start | bytes 1179648 | tf_op jit(solution)/shard_map/all_gather | solution.py:105
  22.1 289.9 %all-reduce.4.cloned.1.call-start = ((), (), s32[]{:S(2)}) async-start(), calls=%async_computation.3 | async-start | bytes 22020096 | tf_op jit(solution)/shard_map/psum | solution.py:122
  43.2 11.5 %copy-start.10 = (bf16[256,2048]{1,0:T(8,128)(2,1)S(1)}, bf16[256,2048]{1,0:T(8,128)(2,1)}, u32[]{:S(2)}) copy-start(bf16[256,2048]{1,0:T(8,128)(2,1)} %all-gather.3.cloned.1.call-done) | copy-start | bytes 3145732
  66.6 11.4 %copy-start.17 = (f32[256,3584]{1,0:T(8,128)S(1)}, f32[256,3584]{1,0:T(8,128)}, u32[]{:S(2)}) copy-start(f32[256,3584]{1,0:T(8,128)} %fusion.88) | copy-start | bytes 11010052
  85.6 332.7 %all-reduce.6.cloned.1.call-start = ((), (), s32[]{:S(2)}) async-start(), calls=%async_computation.5 | async-start | bytes 327680 | tf_op jit(solution)/shard_map/psum | solution.py:225
  88.3 36.9 %copy-start.8 = (bf16[64,3584]{1,0:T(8,128)(2,1)S(1)}, bf16[64,3584]{1,0:T(8,128)(2,1)}, u32[]{:S(2)}) copy-start(bf16[64,3584]{1,0:T(8,128)(2,1)} %param.25) | copy-start | bytes 1376260
  89.8 36.1 %copy-start.12 = (bf16[3584,64]{0,1:T(8,128)(2,1)S(1)}, bf16[3584,64]{0,1:T(8,128)(2,1)}, u32[]{:S(2)}) copy-start(bf16[3584,64]{0,1:T(8,128)(2,1)} %param.28) | copy-start | bytes 1376260
  316.6 9.5 %copy-start.16 = (f32[256,3584]{1,0:T(8,128)S(1)}, f32[256,3584]{1,0:T(8,128)}, u32[]{:S(2)}) copy-start(f32[256,3584]{1,0:T(8,128)} %fusion.2) | copy-start | bytes 11010052
  321.3 4.7 %copy-start.14 = (f32[256,3584]{1,0:T(8,128)S(1)}, f32[256,3584]{1,0:T(8,128)}, u32[]{:S(2)}) copy-start(f32[256,3584]{1,0:T(8,128)} %fusion.61) | copy-start | bytes 11010052
  321.3 5.2 %copy-start.15 = (f32[256,3584]{1,0:T(8,128)S(1)}, f32[256,3584]{1,0:T(8,128)}, u32[]{:S(2)}) copy-start(f32[256,3584]{1,0:T(8,128)} %fusion) | copy-start | bytes 11010052
  336.1 11.2 %copy-start.3 = (bf16[256,3584]{1,0:T(8,128)(2,1)}, bf16[256,3584]{1,0:T(8,128)(2,1)S(1)}, u32[]{:S(2)}) copy-start(bf16[256,3584]{1,0:T(8,128)(2,1)S(1)} %get-tuple-element.9) | copy-start | bytes 5505028
  336.1 26.9 %copy-start.1 = (bf16[256,3584]{1,0:T(8,128)(2,1)}, bf16[256,3584]{1,0:T(8,128)(2,1)S(1)}, u32[]{:S(2)}) copy-start(bf16[256,3584]{1,0:T(8,128)(2,1)S(1)} %get-tuple-element.12) | copy-start | bytes 5505028
  347.2 10.9 %copy-start.13 = (bf16[3584,64]{0,1:T(8,128)(2,1)S(1)}, bf16[3584,64]{0,1:T(8,128)(2,1)}, u32[]{:S(2)}) copy-start(bf16[3584,64]{0,1:T(8,128)(2,1)} %param.28) | copy-start | bytes 1376260
  355.9 5.7 %copy-start.19 = (bf16[64,3584]{1,0:T(8,128)(2,1)S(1)}, bf16[64,3584]{1,0:T(8,128)(2,1)}, u32[]{:S(2)}) copy-start(bf16[64,3584]{1,0:T(8,128)(2,1)} %param.31) | copy-start | bytes 1376260
  360.3 3.9 copy-start.6
  360.3 3.9 copy-start.21
  365.5 92.7 %reduce-scatter.2.cloned.1.call-start = ((), (), s32[]{:S(2)}) async-start(), calls=%async_computation.4 | async-start | bytes 2359296 | tf_op jit(solution)/shard_map/reduce_scatter | solution.py:233
  394.6 23.7 %copy-start.25 = (bf16[2048,64]{0,1:T(8,128)(2,1)S(1)}, bf16[2048,64]{0,1:T(8,128)(2,1)}, u32[]{:S(2)}) copy-start(bf16[2048,64]{0,1:T(8,128)(2,1)} %param.24) | copy-start | bytes 786436
  396.0 25.6 %copy-start.23 = (bf16[2048,64]{0,1:T(8,128)(2,1)S(1)}, bf16[2048,64]{0,1:T(8,128)(2,1)}, u32[]{:S(2)}) copy-start(bf16[2048,64]{0,1:T(8,128)(2,1)} %param.26) | copy-start | bytes 786436
  396.0 26.7 %copy-start.11 = (bf16[256,2048]{1,0:T(8,128)(2,1)S(1)}, bf16[256,2048]{1,0:T(8,128)(2,1)}, u32[]{:S(2)}) copy-start(bf16[256,2048]{1,0:T(8,128)(2,1)} %all-gather.3.cloned.1.call-done) | copy-start | bytes 3145732
  397.4 28.2 %copy-start.27 = (bf16[256,2048]{1,0:T(8,128)(2,1)S(1)}, bf16[256,2048]{1,0:T(8,128)(2,1)}, u32[]{:S(2)}) copy-start(bf16[256,2048]{1,0:T(8,128)(2,1)} %all-gather.5.cloned.1.call-done) | copy-start | bytes 3145732
  418.3 6.2 %copy-start.29 = (bf16[320,256]{1,0:T(8,128)(2,1)S(1)}, bf16[320,256]{1,0:T(8,128)(2,1)}, u32[]{:S(2)}) copy-start(bf16[320,256]{1,0:T(8,128)(2,1)} %all-reduce.6.cloned.1.call-done) | copy-start | bytes 491524
  (11 other events, 26.3 us)
Sparse Core Ops, SparseCore 0:
  21.5 21.6 all-gather.2
  44.8 21.8 all-gather.4
  85.7 226.3 all-reduce.3
  365.7 52.6 all-reduce.5
  420.5 37.6 reduce-scatter.1
where the time goes:
time: 469 us
  waiting for transfers between devices  255 us (54%)
  matrix products  137 us (29%)
  blocking collectives  46.8 us (10%)
  other arithmetic  14.1 us (3%)
  between operations  14.1 us (3%)
    psum x1, waiting for transfers between devices, on_device(): lax.psum(jnp.concatenate([curvature_product(normed_tokens, gate_frozen_we...  178 us
    dot_general x15, matrix products, cross_shard_total(): lax.dot_general(left, right, (((1,), (1,)), ((), ())), preferred_element_...  68.3 us
    dot_general x9, matrix products, curvature_product(): return jnp.dot(left, right, preferred_element_type=jnp.float32)  46.5 us
    psum x1, blocking collectives, on_device(): ranks = lax.psum(projected, 'row').astype(jnp.bfloat16)  35.4 us
    reduce_scatter x1, waiting for transfers between devices, on_device(): lax.psum_scatter(jnp.concatenate([adjoint_contribution, tangent_contribut...  31.5 us
    all_gather x1, waiting for transfers between devices, on_device(): lax.all_gather(own_normed, 'col', axis=0, tiled=True)  21 us
    psum x1, waiting for transfers between devices, on_device(): lax.psum(rank_adjoints.astype(jnp.bfloat16), 'col').astype(jnp.float32)  20.9 us
    psum x1, blocking collectives, on_device(): squares = lax.psum(jnp.sum(tokens_f * tokens_f, axis=1), 'row')  11.4 us
  transfers between devices with their start and end apart: 5, of which 5 were waited for; matrix products, arithmetic and copies ran while one was open for 15% of the time, Pallas kernels for 0%

commit v1 on v0

--- a/solution.py
+++ b/solution.py
@@ -119,17 +119,16 @@
         axis=1,
     )
     ranks = lax.psum(projected, "row").astype(jnp.bfloat16)
-    swiglu_block = lax.psum(
-        jnp.concatenate(
-            [
-                curvature_product(normed_tokens, gate_frozen_weight),
-                curvature_product(normed_tokens, up_frozen_weight),
-                cross_shard_total(cot_panel, down_frozen_weight),
-            ],
-            axis=1,
-        ),
-        "row",
-    )
+    xin = jnp.concatenate(
+        [
+            curvature_product(normed_tokens, gate_frozen_weight),
+            curvature_product(normed_tokens, up_frozen_weight),
+            cross_shard_total(cot_panel, down_frozen_weight),
+        ],
+        axis=1,
+    )
+    piece_now = jax.lax.all_gather(xin, axis_name="row")
+    swiglu_block = jnp.sum(piece_now, axis=0)
 
     def column(array, index):
         return array[:, index * rank_size : (index + 1) * rank_size]

time: 469 us -> 652 us (1.39)
  waiting for transfers between devices: 255 us -> 417 us
  other arithmetic: 14.1 us -> 34.4 us
    all_gather x0 -> x1, waiting for transfers between devices: none -> 344 us  [on_device(): piece_now = jax.lax.all_gather(xin, axis_name='row')]
    psum x1 -> x0, waiting for transfers between devices: 178 us -> none  [on_device(): lax.psum(jnp.concatenate([curvature_product(normed_tokens, gate_frozen_we...]
    reduce_sum x0 -> x1, other arithmetic: none -> 20.3 us  [on_device(): swiglu_block = jnp.sum(piece_now, axis=0)]
  transfers between devices with their start and end apart: 5 -> 5, of which waited for: 5 -> 5; matrix products, arithmetic and copies ran while one was open for 15% -> 12% of each run, Pallas kernels for 0% -> 0%
where the time goes in v1:
time: 652 us; the launch traced here: 651 us
  waiting for transfers between devices  417 us (64%)
  matrix products  143 us (22%)
  blocking collectives  40.3 us (6%)
  other arithmetic  34.4 us (5%)
  between operations  14.1 us (2%)
    all_gather x1, waiting for transfers between devices, on_device(): piece_now = jax.lax.all_gather(xin, axis_name='row')  344 us
    dot_general x15, matrix products, cross_shard_total(): lax.dot_general(left, right, (((1,), (1,)), ((), ())), preferred_element_...  74.8 us
    dot_general x9, matrix products, curvature_product(): return jnp.dot(left, right, preferred_element_type=jnp.float32)  46.4 us
    reduce_scatter x1, waiting for transfers between devices, on_device(): lax.psum_scatter(jnp.concatenate([adjoint_contribution, tangent_contribut...  31.4 us
    psum x1, blocking collectives, on_device(): ranks = lax.psum(projected, 'row').astype(jnp.bfloat16)  28.9 us
    all_gather x1, waiting for transfers between devices, on_device(): lax.all_gather(own_normed, 'col', axis=0, tiled=True)  21 us
    reduce_sum x1, other arithmetic, on_device(): swiglu_block = jnp.sum(piece_now, axis=0)  20.3 us
    psum x1, waiting for transfers between devices, on_device(): lax.psum(rank_adjoints.astype(jnp.bfloat16), 'col').astype(jnp.float32)  16.6 us
  transfers between devices with their start and end apart: 5, of which 5 were waited for; matrix products, arithmetic and copies ran while one was open for 12% of the time, Pallas kernels for 0%

profile of v1, /device:TPU:0, one launch (start us, length us, event | category | flops | bytes accessed | tf_op | source)
XLA Modules:
  0.0 651.4 jit_solution(5762324495696623502)
XLA Ops:
  8.3 11.4 %psum.21 = f32[32]{0:T(128)S(1)} all-reduce(f32[32]{0:T(128)S(1)} %fusion.49), channel_id=1, replica_groups=mesh['row'=4,'col'=8] {'row'}, use_global_device_ids=true, to_apply=%region_1.0 | all-reduce | flops 32 | bytes 256 | tf_op jit(solution)/shard_map/psum | solution.py:99
  22.2 21.0 %all-gather.5.cloned.1.call-done = bf16[256,2048]{1,0:T(8,128)(2,1)} async-done(((bf16[32,2048]{1,0:T(8,128)(2,1)}), bf16[256,2048]{1,0:T(8,128)(2,1)}) %all-gather.5.cloned.1.call-update) | async-done | bytes 1048592 | tf_op jit(solution)/shard_map/all_gather | solution.py:104
  43.2 11.5 %fusion.89 = f32[256,3584]{1,0:T(8,128)} fusion(bf16[256,2048]{1,0:T(8,128)(2,1)} %all-gather.5.cloned.1.call-done, bf16[2048,3584]{1,0:T(8,128)(2,1)} %param.22), kind=kOutput, calls=%fused_computation.127 | convolution fusion | flops 3758096384 | bytes 19398656 | tf_op jit(solution)/shard_map/dot_general | solution.py:12
  54.6 9.1 %fusion.88 = f32[256,3584]{1,0:T(8,128)} fusion(bf16[256,2048]{1,0:T(8,128)(2,1)S(1)} %copy-done.10, bf16[2048,3584]{1,0:T(8,128)(2,1)} %param.21), kind=kOutput, calls=%fused_computation.126 | convolution fusion | flops 3758096384 | bytes 19398656 | tf_op jit(solution)/shard_map/dot_general | solution.py:12
  63.8 2.8 all-gather.7.cloned.1.call-done
  66.6 11.4 %fusion.90 = f32[256,3584]{1,0:T(8,128)} fusion(bf16[256,2048]{1,0:T(8,128)(2,1)} %all-gather.7.cloned.1.call-done, bf16[3584,2048]{1,0:T(8,128)(2,1)} %param.23), kind=kOutput, calls=%fused_computation.128 | convolution fusion | flops 3758096384 | bytes 19398656 | tf_op jit(solution)/shard_map/dot_general | solution.py:16
  78.0 7.5 %pad_maximum_fusion = f32[256,10752]{1,0:T(8,128)} fusion(f32[256,3584]{1,0:T(8,128)} %fusion.90, f32[256,3584]{1,0:T(8,128)S(1)} %copy-done.16, f32[256,3584]{1,0:T(8,128)} %fusion.88), kind=kLoop, calls=%fused_computation | loop fusion | flops 5505024 | bytes 22020096 | tf_op jit(solution)/shard_map/concatenate | solution.py:122
  89.9 28.9 %all-reduce.4 = bf16[256,384]{0,1:T(8,128)(2,1)S(1)} all-reduce(f32[256,384]{0,1:T(8,128)S(1)} %pad_maximum_fusion.2), channel_id=1, replica_groups=mesh['row'=4,'col'=8] {'row'}, use_global_device_ids=true, to_apply=%region_3.0 | all-reduce | flops 98304 | bytes 589824 | tf_op jit(solution)/shard_map/psum | solution.py:121
  120.2 2.4 fusion.61
  122.6 2.4 fusion
  125.1 2.5 fusion.2
  127.6 343.9 %all-gather.9.cloned.1.call-done = f32[1024,10752]{1,0:T(8,128)} async-done(((f32[256,10752]{1,0:T(8,128)}), f32[1024,10752]{1,0:T(8,128)}) %all-gather.9.cloned.1.call-update) | async-done | bytes 44040208 | tf_op jit(solution)/shard_map/all_gather | solution.py:130
  471.4 20.3 %reduce_sum.19 = f32[256,10752]{1,0:T(8,128)} reduce(f32[4,256,10752]{2,1,0:T(8,128)} %bitcast.79, f32[]{:T(128)} %constant.10.clone.1), dimensions={0}, to_apply=%region_2.0 | reduce | flops 8257536 | bytes 55050244 | tf_op jit(solution)/shard_map/reduce_sum | solution.py:131
  491.8 4.5 fusion.4
  496.3 4.5 fusion.3
  500.8 4.8 fusion.5
  506.0 9.7 %add_convert_fusion = (bf16[256,3584]{1,0:T(8,128)(2,1)}, bf16[256,3584]{1,0:T(8,128)(2,1)S(1)}, bf16[256,3584]{1,0:T(8,128)(2,1)}, bf16[256,3584]{1,0:T(8,128)(...) fusion(f32[256,3584]{1,0:T(8,128)} %fusion.4, f32[256,3584]{1,0:T(8,128)S(1)} %copy-done.15, ...), kind=kOutput, calls=%fused_computation.31 | convolution fusion | flops 155975680 | bytes 33521664 | tf_op jit(solution)/shard_map/dot_general | solution.py:12
  517.7 11.0 %fusion.92 = f32[256,2048]{1,0:T(8,128)} fusion(bf16[256,3584]{1,0:T(8,128)(2,1)} %copy-done.5, bf16[2048,3584]{1,0:T(8,128)(2,1)} %param.21), kind=kOutput, calls=%fused_computation.130 | convolution fusion | flops 3758096384 | bytes 18612224 | tf_op jit(solution)/shard_map/dot_general | solution.py:16
  530.0 8.7 %fusion.91 = f32[256,2048]{1,0:T(8,128)} fusion(bf16[256,3584]{1,0:T(8,128)(2,1)S(1)} %get-tuple-element.11, bf16[2048,3584]{1,0:T(8,128)(2,1)} %param.21), kind=kOutput, calls=%fused_computation.129 | convolution fusion | flops 3758096384 | bytes 18612224 | tf_op jit(solution)/shard_map/dot_general | solution.py:16
  548.3 10.3 %fusion.20 = bf16[256,2048]{1,0:T(8,128)(2,1)S(1)} fusion(f32[256,2048]{1,0:T(8,128)} %fusion.92, bf16[256,3584]{1,0:T(8,128)(2,1)} %get-tuple-element.10, bf16[2048,3584]{1,0:T(8,128)(2,1)} %param.22), kind=kOutput, calls=%fused_computation.40 | convolution fusion | flops 3759144960 | bytes 19660800 | tf_op jit(solution)/shard_map/dot_general | solution.py:16
  558.6 15.9 %fusion.19 = bf16[256,2048]{1,0:T(8,128)(2,1)} fusion(f32[256,2048]{1,0:T(8,128)} %fusion.91, bf16[256,3584]{1,0:T(8,128)(2,1)S(1)} %get-tuple-element.12, bf16[2048,3584]{1,0:T(8,128)(2,1)} %param.22), kind=kOutput, calls=%fused_computation.39 | convolution fusion | flops 3759144960 | bytes 19660800 | tf_op jit(solution)/shard_map/dot_general | solution.py:16
  574.5 2.8 pad_maximum_fusion.1
  584.5 16.6 %all-reduce.3.cloned.1.call-done = bf16[320,256]{1,0:T(8,128)(2,1)} async-done(((bf16[320,256]{1,0:T(8,128)(2,1)}), bf16[320,256]{1,0:T(8,128)(2,1)}) %all-reduce.3.cloned.1.call-update) | async-done | bytes 163856 | tf_op jit(solution)/shard_map/psum | solution.py:224
  609.5 31.4 %reduce-scatter.2.cloned.1.call-done = bf16[32,4096]{1,0:T(8,128)(2,1)} async-done(((bf16[256,4096]{1,0:T(8,128)(2,1)}), bf16[32,4096]{1,0:T(8,128)(2,1)}) %reduce-scatter.2.cloned.1.call-update) | async-done | bytes 262160 | tf_op jit(solution)/shard_map/reduce_scatter | solution.py:232
  (100 shorter events, 41.9 us)
Async XLA Ops:
  7.2 498.4 %copy-start = (bf16[64,3584]{1,0:T(8,128)(2,1)S(1)}, bf16[64,3584]{1,0:T(8,128)(2,1)}, u32[]{:S(2)}) copy-start(bf16[64,3584]{1,0:T(8,128)(2,1)} %param.33) | copy-start | bytes 1376260
  7.2 36.0 %all-gather.5.cloned.1.call-start = ((), (), s32[]{:S(2)}) async-start(), calls=%async_computation.1 | async-start | bytes 1179648 | tf_op jit(solution)/shard_map/all_gather | solution.py:104
  21.4 45.2 %all-gather.7.cloned.1.call-start = ((), (), s32[]{:S(2)}) async-start(), calls=%async_computation.2 | async-start | bytes 1179648 | tf_op jit(solution)/shard_map/all_gather | solution.py:105
  22.1 449.3 %all-gather.9.cloned.1.call-start = ((), (), s32[]{:S(2)}) async-start(), calls=%async_computation.5 | async-start | bytes 55050240 | tf_op jit(solution)/shard_map/all_gather | solution.py:130
  43.2 11.5 %copy-start.10 = (bf16[256,2048]{1,0:T(8,128)(2,1)S(1)}, bf16[256,2048]{1,0:T(8,128)(2,1)}, u32[]{:S(2)}) copy-start(bf16[256,2048]{1,0:T(8,128)(2,1)} %all-gather.5.cloned.1.call-done) | copy-start | bytes 3145732
  66.6 11.4 %copy-start.16 = (f32[256,3584]{1,0:T(8,128)S(1)}, f32[256,3584]{1,0:T(8,128)}, u32[]{:S(2)}) copy-start(f32[256,3584]{1,0:T(8,128)} %fusion.89) | copy-start | bytes 11010052
  85.6 515.5 %all-reduce.3.cloned.1.call-start = ((), (), s32[]{:S(2)}) async-start(), calls=%async_computation.4 | async-start | bytes 327680 | tf_op jit(solution)/shard_map/psum | solution.py:224
  88.3 30.5 %copy-start.8 = (bf16[64,3584]{1,0:T(8,128)(2,1)S(1)}, bf16[64,3584]{1,0:T(8,128)(2,1)}, u32[]{:S(2)}) copy-start(bf16[64,3584]{1,0:T(8,128)(2,1)} %param.25) | copy-start | bytes 1376260
  89.8 29.7 %copy-start.12 = (bf16[3584,64]{0,1:T(8,128)(2,1)S(1)}, bf16[3584,64]{0,1:T(8,128)(2,1)}, u32[]{:S(2)}) copy-start(bf16[3584,64]{0,1:T(8,128)(2,1)} %param.28) | copy-start | bytes 1376260
  119.5 3.1 copy-start.17
  500.8 4.8 copy-start.14
  500.8 5.2 copy-start.15
  515.8 28.6 %copy-start.1 = (bf16[256,3584]{1,0:T(8,128)(2,1)}, bf16[256,3584]{1,0:T(8,128)(2,1)S(1)}, u32[]{:S(2)}) copy-start(bf16[256,3584]{1,0:T(8,128)(2,1)S(1)} %get-tuple-element.11) | copy-start | bytes 5505028
  515.8 31.2 %copy-start.2 = (bf16[256,3584]{1,0:T(8,128)(2,1)}, bf16[256,3584]{1,0:T(8,128)(2,1)S(1)}, u32[]{:S(2)}) copy-start(bf16[256,3584]{1,0:T(8,128)(2,1)S(1)} %get-tuple-element.13) | copy-start | bytes 5505028
  530.0 10.9 %copy-start.13 = (bf16[3584,64]{0,1:T(8,128)(2,1)S(1)}, bf16[3584,64]{0,1:T(8,128)(2,1)}, u32[]{:S(2)}) copy-start(bf16[3584,64]{0,1:T(8,128)(2,1)} %param.28) | copy-start | bytes 1376260
  538.6 5.7 copy-start.18
  543.0 3.9 copy-start.20
  548.2 92.7 %reduce-scatter.2.cloned.1.call-start = ((), (), s32[]{:S(2)}) async-start(), calls=%async_computation.3 | async-start | bytes 2359296 | tf_op jit(solution)/shard_map/reduce_scatter | solution.py:232
  577.3 3.0 copy-start.6
  581.7 19.4 %copy-start.24 = (bf16[2048,64]{0,1:T(8,128)(2,1)S(1)}, bf16[2048,64]{0,1:T(8,128)(2,1)}, u32[]{:S(2)}) copy-start(bf16[2048,64]{0,1:T(8,128)(2,1)} %param.24) | copy-start | bytes 786436
  583.1 21.3 %copy-start.22 = (bf16[2048,64]{0,1:T(8,128)(2,1)S(1)}, bf16[2048,64]{0,1:T(8,128)(2,1)}, u32[]{:S(2)}) copy-start(bf16[2048,64]{0,1:T(8,128)(2,1)} %param.26) | copy-start | bytes 786436
  583.1 22.4 %copy-start.11 = (bf16[256,2048]{1,0:T(8,128)(2,1)S(1)}, bf16[256,2048]{1,0:T(8,128)(2,1)}, u32[]{:S(2)}) copy-start(bf16[256,2048]{1,0:T(8,128)(2,1)} %all-gather.5.cloned.1.call-done) | copy-start | bytes 3145732
  584.5 24.0 %copy-start.26 = (bf16[256,2048]{1,0:T(8,128)(2,1)S(1)}, bf16[256,2048]{1,0:T(8,128)(2,1)}, u32[]{:S(2)}) copy-start(bf16[256,2048]{1,0:T(8,128)(2,1)} %all-gather.7.cloned.1.call-done) | copy-start | bytes 3145732
  601.1 6.2 copy-start.28
  (10 other events, 21.7 us)
Sparse Core Ops, SparseCore 0:
  21.5 21.6 all-gather.4
  44.8 21.8 all-gather.6
  85.7 385.6 all-gather.8
  548.4 52.6 all-reduce.2
  603.2 37.6 reduce-scatter.1
